TPU v7x, 32 devices: a whole 2x2x4 slice. The times are simulated.
32 devices in a mesh: blk: 8 (over z, x), head: 4 (over y, core).
Axes of the slice: x: 2, y: 2, z: 4, core: 2. Of those that a mesh axis runs over, the one named last changes fastest.
Arguments:
- queries: bfloat16 [4096, 1024], P(('blk', 'head')), may hold values from -6 to 6
- key_vectors: bfloat16 [4096, 1024], P(('blk', 'head')), may hold values from -6 to 6
- value_vectors: bfloat16 [4096, 1024], P(('blk', 'head')), may hold values from -6 to 6
- grad_output: bfloat16 [4096, 1024], P(('blk', 'head')), may hold values from -6 to 6
- lengths: int32 [4], replicated, may hold values from 1 to 2048, 4096 in all
Outputs:
- grad_queries: bfloat16 [4096, 1024], P(('blk', 'head'))
- grad_keys: bfloat16 [4096, 1024], P(('blk', 'head'))
- grad_values: bfloat16 [4096, 1024], P(('blk', 'head'))
Inputs may be any that keep to these rules, and one draw needn't show every extreme that they name: 4 positive lengths that sum to 4096; the longest is exactly 2048.
All inputs are finite; a program needn't handle non-finite values.
Results may differ from a plain program's by a relative error of at most 0.0086.
Values may be sent and summed in bfloat16 or wider, within the bound.
No kernel may reach another device: no remote copies, remote signals or barrier semaphores. Data moves between devices by JAX's collectives and lax.ppermute only.
A program may use at most 64 MiB of HBM per device.

v0:
```python
import jax
import jax.numpy as jnp
from jax import lax
from jax.sharding import PartitionSpec as P

DH = 64
WIN = 64


def with_halo(block, sides, width):
    for axis, dim in sides:
        count = lax.axis_size(axis)
        forward = [(i, i + 1) for i in range(count - 1)]
        backward = [(target, source) for source, target in forward]
        low = lax.ppermute(
            lax.slice_in_dim(block, block.shape[dim] - width, None, axis=dim), axis, forward
        )
        high = lax.ppermute(lax.slice_in_dim(block, 0, width, axis=dim), axis, backward)
        block = jnp.concatenate([low, block, high], axis=dim)
    return block


def shifted(block, axis, distance):
    devices = range(lax.axis_size(axis))
    route = [(i - distance, i) for i in devices if i - distance in devices]
    return lax.ppermute(block, axis, route)


def recording_of(positions, rec_ends):
    return jnp.sum((rec_ends[None, :] <= positions[:, None]).astype(jnp.int32), axis=1)


def band_grads(query_rows, grad_rows, key_value, query_first, key_first, rec_ends, frames):
    row_count = query_rows.shape[0]
    columns = query_rows.shape[1]
    head_count = columns // DH
    step_rows = min(512, 2 * WIN)
    key_span = step_rows + 2 * WIN
    score_scale = DH ** (-0.5)
    pair_grad = jnp.zeros((key_value.shape[0], 2 * columns), jnp.float32)
    query_parts = []
    for first_row in range(0, row_count, step_rows):
        query_block = query_rows[first_row : first_row + step_rows].reshape(
            step_rows, head_count, DH
        )
        grad_block = grad_rows[first_row : first_row + step_rows].reshape(step_rows, head_count, DH)
        pair_block = key_value[first_row : first_row + key_span]
        key_block = pair_block[:, :columns].reshape(key_span, head_count, DH)
        value_block = pair_block[:, columns:].reshape(key_span, head_count, DH)
        query_pos = query_first + first_row + jnp.arange(step_rows, dtype=jnp.int32)
        key_pos = key_first + first_row + jnp.arange(key_span, dtype=jnp.int32)
        inside = (key_pos >= 0) & (key_pos < frames)
        visible = jnp.abs(query_pos[:, None] - key_pos[None, :]) <= WIN
        visible = visible & (
            recording_of(query_pos, rec_ends)[:, None] == recording_of(key_pos, rec_ends)[None, :]
        )
        visible = visible & (inside[None, :] | (query_pos[:, None] == key_pos[None, :]))
        scores = (
            jnp.einsum("qhd,khd->hqk", query_block, key_block, preferred_element_type=jnp.float32)
            * score_scale
        )
        scores = jnp.where(visible[None], scores, -1e30)
        row_max = jnp.max(scores, axis=-1, keepdims=True)
        weights = jnp.where(visible[None], jnp.exp(scores - row_max), 0.0)
        probs = weights / jnp.sum(weights, axis=-1, keepdims=True)
        probs_low = probs.astype(jnp.bfloat16)
        value_part = jnp.einsum(
            "hqk,qhd->khd", probs_low, grad_block, preferred_element_type=jnp.float32
        )
        prob_grad = jnp.einsum(
            "qhd,khd->hqk", grad_block, value_block, preferred_element_type=jnp.float32
        )
        row_delta = jnp.sum(probs * prob_grad, axis=-1, keepdims=True)
        score_grad = (probs * (prob_grad - row_delta) * score_scale).astype(jnp.bfloat16)
        query_grad = jnp.einsum(
            "hqk,khd->qhd", score_grad, key_block, preferred_element_type=jnp.float32
        )
        key_part = jnp.einsum(
            "hqk,qhd->khd", score_grad, query_block, preferred_element_type=jnp.float32
        )
        both_parts = jnp.concatenate(
            [key_part.reshape(key_span, columns), value_part.reshape(key_span, columns)], axis=1
        )
        pair_grad = pair_grad.at[first_row : first_row + key_span].add(both_parts)
        query_parts.append(query_grad.reshape(step_rows, columns))
    return (jnp.concatenate(query_parts, axis=0), pair_grad)


def body(queries, key_vectors, value_vectors, grad_output, lengths):
    group_size = lax.axis_size("head")
    block_rows = queries.shape[0] * group_size
    columns = queries.shape[1] // group_size
    frames = block_rows * lax.axis_size("blk")
    head_queries, head_keys, head_values, head_grads = (
        lax.all_to_all(queries, "head", split_axis=1, concat_axis=0, tiled=True),
        lax.all_to_all(key_vectors, "head", split_axis=1, concat_axis=0, tiled=True),
        lax.all_to_all(value_vectors, "head", split_axis=1, concat_axis=0, tiled=True),
        lax.all_to_all(grad_output, "head", split_axis=1, concat_axis=0, tiled=True),
    )
    key_value = jnp.concatenate([head_keys, head_values], axis=1)
    rec_ends = jnp.cumsum(lengths)
    base_pos = lax.axis_index("blk") * block_rows
    extended = with_halo(key_value, (("blk", 0),), WIN)
    query_grad, pair_grad = band_grads(
        head_queries, head_grads, extended, base_pos, base_pos - WIN, rec_ends, frames
    )
    own_rows = pair_grad[WIN : WIN + block_rows]
    arrived = []
    for step_by, rim_rows in ((1, pair_grad[WIN + block_rows :]), (-1, pair_grad[:WIN])):
        arrived.append(shifted(rim_rows, "blk", step_by))
    own_rows = own_rows.at[:WIN].add(arrived[0]).at[block_rows - WIN :].add(arrived[1])
    outputs = (
        lax.all_to_all(
            query_grad.astype(jnp.bfloat16), "head", split_axis=0, concat_axis=1, tiled=True
        ),
        lax.all_to_all(
            own_rows[:, :columns].astype(jnp.bfloat16),
            "head",
            split_axis=0,
            concat_axis=1,
            tiled=True,
        ),
        lax.all_to_all(
            own_rows[:, columns:].astype(jnp.bfloat16),
            "head",
            split_axis=0,
            concat_axis=1,
            tiled=True,
        ),
    )
    return (outputs[0], outputs[1], outputs[2])


def solution(mesh):
    return jax.shard_map(
        body,
        mesh=mesh,
        in_specs=(
            P(("blk", "head"), None),
            P(("blk", "head"), None),
            P(("blk", "head"), None),
            P(("blk", "head"), None),
            P(),
        ),
        out_specs=(P(("blk", "head"), None), P(("blk", "head"), None), P(("blk", "head"), None)),
        check_vma=False,
    )
```

profile of v0, /device:TPU:26, one launch (start us, length us, event | category | flops | bytes accessed | tf_op | source)
XLA Modules:
  0.0 104.3 jit_solution(3987964290970095193)
XLA Ops:
  0.7 1.2 %copy.101 = bf16[128,1024]{0,1:T(8,128)(2,1)S(1)} copy(bf16[128,1024]{1,0:T(8,128)(2,1)} %param.18) | data formatting | bytes 524288 | tf_op args[1]
  1.8 0.9 copy.102
  2.7 3.4 %all-to-all-start = ((bf16[128,4,256]{2,0,1:T(8,128)(2,1)}), bf16[128,4,256]{2,0,1:T(8,128)(2,1)S(1)}, u32[]{:S(2)}, u32[]{:S(2)}) async-start(bf16[128,4,256]{2,0,1:T(8,128)(2,1)} %copy.102), calls=%async_computation | async-start | bytes 524288 | tf_op jit(solution)/shard_map/all_to_all | solution.py:96
  6.2 0.8 copy.156
  7.2 0.9 copy.104
  8.6 0.8 fusion.86
  9.4 2.7 %all-to-all-done = bf16[128,4,256]{2,0,1:T(8,128)(2,1)S(1)} async-done(((bf16[128,4,256]{2,0,1:T(8,128)(2,1)}), bf16[128,4,256]{2,0,1:T(8,128)(2,1)S(1)}, u32[]{:S(2)}, u32[]{:S(2)}) %all-to-all-start) | async-done | bytes 262176 | tf_op jit(solution)/shard_map/all_to_all | solution.py:96
  12.1 3.4 %all-to-all-start.1 = ((bf16[128,4,256]{2,0,1:T(8,128)(2,1)}), bf16[128,4,256]{2,0,1:T(8,128)(2,1)S(1)}, u32[]{:S(2)}, u32[]{:S(2)}) async-start(bf16[128,4,256]{2,0,1:T(8,128)(2,1)} %copy.104), calls=%async_computation.1 | async-start | bytes 524288 | tf_op jit(solution)/shard_map/all_to_all | solution.py:97
  15.5 0.8 fusion.85
  16.3 5.2 %all-to-all-done.1 = bf16[128,4,256]{2,0,1:T(8,128)(2,1)S(1)} async-done(((bf16[128,4,256]{2,0,1:T(8,128)(2,1)}), bf16[128,4,256]{2,0,1:T(8,128)(2,1)S(1)}, u32[]{:S(2)}, u32[]{:S(2)}) %all-to-all-start.1) | async-done | bytes 262176 | tf_op jit(solution)/shard_map/all_to_all | solution.py:97
  21.5 3.4 %all-to-all-start.2 = ((bf16[128,4,256]{0,2,1:T(8,128)(2,1)}), bf16[128,4,256]{0,2,1:T(8,128)(2,1)S(1)}, u32[]{:S(2)}, u32[]{:S(2)}) async-start(bf16[128,4,256]{0,2,1:T(8,128)(2,1)} %bitcast.9), calls=%async_computation.2 | async-start | bytes 524288 | tf_op jit(solution)/shard_map/all_to_all | solution.py:95
  25.1 0.8 copy.157
  26.4 1.3 %collective-permute-start = (bf16[64,512]{0,1:T(8,128)(2,1)S(1)}, bf16[64,512]{0,1:T(8,128)(2,1)S(1)}, u32[]{:S(2)}, u32[]{:S(2)}) collective-permute-start(bf16[64,512]{0,1:T(8,128)(2,1)S(1)} %get-tuple-element.101), channel_id=1, source_target_pairs={{0,4},{4,8},{8,12},{12,16},{16,20},{20,24},{24,28},{1,5},{5,9},{9,... | collective-permute-start | bytes 196616 | tf_op jit(solution)/shard_map/ppermute | solution.py:15
  27.7 4.6 %collective-permute-start.1 = (bf16[64,512]{0,1:T(8,128)(2,1)S(1)}, bf16[64,512]{0,1:T(8,128)(2,1)S(1)}, u32[]{:S(2)}, u32[]{:S(2)}) collective-permute-start(bf16[64,512]{0,1:T(8,128)(2,1)S(1)} %get-tuple-element.102), channel_id=1, source_target_pairs={{4,0},{8,4},{12,8},{16,12},{20,16},{24,20},{28,24},{5,1},{9,5},{13... | collective-permute-start | bytes 196616 | tf_op jit(solution)/shard_map/ppermute | solution.py:18
  32.2 3.4 %all-to-all-start.3 = ((bf16[128,4,256]{0,2,1:T(8,128)(2,1)}), bf16[128,4,256]{0,2,1:T(8,128)(2,1)S(1)}, u32[]{:S(2)}, u32[]{:S(2)}) async-start(bf16[128,4,256]{0,2,1:T(8,128)(2,1)} %bitcast.14), calls=%async_computation.3 | async-start | bytes 524288 | tf_op jit(solution)/shard_map/all_to_all | solution.py:98
  35.7 6.0 %all-to-all-done.3 = bf16[128,4,256]{0,2,1:T(8,128)(2,1)S(1)} async-done(((bf16[128,4,256]{0,2,1:T(8,128)(2,1)}), bf16[128,4,256]{0,2,1:T(8,128)(2,1)S(1)}, u32[]{:S(2)}, u32[]{:S(2)}) %all-to-all-start.3) | async-done | bytes 262176 | tf_op jit(solution)/shard_map/all_to_all | solution.py:98
  41.7 0.5 pad_maximum_fusion.5
  43.0 0.9 convolution_convert_fusion.3
  44.2 0.6 fusion.70
  45.4 0.9 convolution_convert_fusion.2
  46.4 1.0 fusion.45
  47.4 1.3 %fusion.64 = f32[4,256,64]{1,2,0:T(8,128)} fusion(bf16[128,4,64]{0,2,1:T(8,128)(2,1)S(1)} %bitcast.172, f32[4,128]{1,0:T(4,128)S(1)} %get-tuple-element.115, pred[128,256]{0,1:T(8,128)(4,1)S(1)} %fusion.84, bf16[256,4,64]{0,2,1:T(8,128)(2,1)S(1)} %bitcast.183, bf16[128,4,64]{0,2,1:T(8,128)(2,1)S(1)} %bitcast.197), kind=kOutput, calls=%fused_computation.78 | convolution fusion | flops 34341632 | bytes 559104 | tf_op jit(solution)/shard_map/hqk,qhd->khd/dot_general | solution.py:67
  48.9 1.2 %fusion.121 = (f32[4,128]{1,0:T(4,128)S(1)}, f32[4,128,256]{1,2,0:T(8,128)}) fusion(bf16[128,4,64]{0,2,1:T(8,128)(2,1)S(1)} %bitcast.191, bf16[256,4,64]{0,2,1:T(8,128)(2,1)S(1)} %bitcast.178, pred[128,256]{0,1:T(8,128)(4,1)S(1)} %copy-done.16), kind=kOutput, calls=%fused_computation.172 | convolution fusion | flops 17432832 | bytes 755712 | tf_op jit(solution)/shard_map/sub | solution.py:64
  50.1 0.6 fusion.66
  51.4 1.3 %fusion.68 = f32[4,256,64]{1,2,0:T(8,128)} fusion(bf16[128,4,64]{0,2,1:T(8,128)(2,1)S(1)} %bitcast.168, f32[4,128]{1,0:T(4,128)S(1)} %get-tuple-element.119, pred[128,256]{0,1:T(8,128)(4,1)S(1)} %copy-done.15, bf16[128,4,64]{0,2,1:T(8,128)(2,1)S(1)} %bitcast.189, bf16[256,4,64]{0,2,1:T(8,128)(2,1)S(1)} %bitcast.176), kind=kOutput, calls=%fused_computation.82 | convolution fusion | flops 34341632 | bytes 559104 | tf_op jit(solution)/shard_map/hqk,qhd->khd/dot_general | solution.py:67
  52.7 1.5 %fusion.44 = f32[4,256,64]{1,2,0:T(8,128)S(1)} fusion(bf16[128,4,64]{0,2,1:T(8,128)(2,1)S(1)} %bitcast.193, f32[4,128,256]{1,2,0:T(8,128)S(1)} %fusion.125, f32[4,128,256]{1,2,0:T(8,128)} %get-tuple-element.118, f32[4,128]{1,0:T(4,128)S(1)} %get-tuple-element.117), kind=kOutput, calls=%fused_computation.56 | convolution fusion | flops 17695488 | bytes 1378304 | tf_op jit(solution)/shard_map/hqk,qhd->khd/dot_general | solution.py:78
  54.3 1.0 fusion.43
  55.4 0.9 copy-done.3
  56.5 0.7 copy-done.5
  57.6 1.3 %collective-permute-start.2 = (f32[64,512]{0,1:T(8,128)S(1)}, f32[64,512]{0,1:T(8,128)S(1)}, u32[]{:S(2)}, u32[]{:S(2)}) collective-permute-start(f32[64,512]{0,1:T(8,128)S(1)} %slice.255), channel_id=1, source_target_pairs={{0,4},{4,8},{8,12},{12,16},{16,20},{20,24},{24,28},{1,5},{5,9},{9,... | collective-permute-start | bytes 393224 | tf_op jit(solution)/shard_map/ppermute | solution.py:26
  59.0 1.5 %convolution_convert_fusion = bf16[4,128,64]{1,2,0:T(8,128)(2,1)S(1)} fusion(bf16[256,4,64]{0,2,1:T(8,128)(2,1)S(1)} %bitcast.180, f32[4,128,256]{1,2,0:T(8,128)S(1)} %fusion.125, f32[4,128,256]{1,2,0:T(8,128)} %get-tuple-element.118, f32[4,128]{1,0:T(4,128)S(1)} %get-tuple-element.117), kind=kOutput, calls=%fused_computation.50 | convolution fusion | flops 17728256 | bytes 1247232 | tf_op jit(solution)/shard_map/hqk,khd->qhd/dot_general | solution.py:75
  60.5 6.9 %collective-permute-done.2 = f32[64,512]{0,1:T(8,128)S(1)} collective-permute-done((f32[64,512]{0,1:T(8,128)S(1)}, f32[64,512]{0,1:T(8,128)S(1)}, u32[]{:S(2)}, u32[]{:S(2)}) %collective-permute-start.2) | collective-permute-done | bytes 131104 | tf_op jit(solution)/shard_map/ppermute | solution.py:26
  67.5 4.2 %collective-permute-start.3 = (f32[64,512]{0,1:T(8,128)S(1)}, f32[64,512]{0,1:T(8,128)S(1)}, u32[]{:S(2)}, u32[]{:S(2)}) collective-permute-start(f32[64,512]{0,1:T(8,128)S(1)} %get-tuple-element.91), channel_id=1, source_target_pairs={{4,0},{8,4},{12,8},{16,12},{20,16},{24,20},{28,24},{5,1},{9,5},{13... | collective-permute-start | bytes 393224 | tf_op jit(solution)/shard_map/ppermute | solution.py:26
  71.8 1.5 %convolution_convert_fusion.1 = bf16[4,128,64]{1,2,0:T(8,128)(2,1)S(1)} fusion(bf16[256,4,64]{0,2,1:T(8,128)(2,1)S(1)} %bitcast.177, f32[4,128,256]{1,2,0:T(8,128)S(1)} %fusion.124, f32[4,128,256]{1,2,0:T(8,128)} %copy-done.18, f32[4,128]{1,0:T(4,128)S(1)} %get-tuple-element.119), kind=kOutput, calls=%fused_computation.51 | convolution fusion | flops 17728256 | bytes 1247232 | tf_op jit(solution)/shard_map/hqk,khd->qhd/dot_general | solution.py:75
  74.2 0.8 copy.123
  75.0 3.4 %all-to-all-start.4 = ((bf16[4,128,256]{2,1,0:T(8,128)(2,1)}), bf16[4,128,256]{2,1,0:T(8,128)(2,1)S(1)}, u32[]{:S(2)}, u32[]{:S(2)}) async-start(bf16[4,128,256]{2,1,0:T(8,128)(2,1)} %bitcast.42), calls=%async_computation.4 | async-start | bytes 524288 | tf_op jit(solution)/shard_map/all_to_all | solution.py:113
  78.5 1.9 %scatter-add.26 = f32[512,512]{0,1:T(8,128)S(1)} dynamic-update-slice(f32[512,512]{0,1:T(8,128)S(1)} %slice.253, f32[64,512]{0,1:T(8,128)S(1)} %get-tuple-element.92, s32[]{:T(128)} %constant.187.clone.1, s32[]{:T(128)} %constant.187.clone.1) | dynamic-update-slice | bytes 262148 | tf_op jit(solution)/shard_map/scatter-add | solution.py:111
  80.5 1.5 %scatter-add.29 = f32[512,512]{0,1:T(8,128)S(1)} dynamic-update-slice(f32[512,512]{0,1:T(8,128)S(1)} %scatter-add.26, f32[64,512]{0,1:T(8,128)S(1)} %slice_add_fusion.3, s32[]{:T(128)} %constant.198.clone.1, s32[]{:T(128)} %constant.187.clone.1) | dynamic-update-slice | bytes 262148 | tf_op jit(solution)/shard_map/scatter-add | solution.py:111
  82.1 0.8 copy.135
  83.0 1.5 %all-to-all-done.4 = bf16[4,128,256]{2,1,0:T(8,128)(2,1)S(1)} async-done(((bf16[4,128,256]{2,1,0:T(8,128)(2,1)}), bf16[4,128,256]{2,1,0:T(8,128)(2,1)S(1)}, u32[]{:S(2)}, u32[]{:S(2)}) %all-to-all-start.4) | async-done | bytes 262176 | tf_op jit(solution)/shard_map/all_to_all | solution.py:113
  84.5 3.4 %all-to-all-start.6 = ((bf16[4,128,256]{2,1,0:T(8,128)(2,1)}), bf16[4,128,256]{2,1,0:T(8,128)(2,1)S(1)}, u32[]{:S(2)}, u32[]{:S(2)}) async-start(bf16[4,128,256]{2,1,0:T(8,128)(2,1)} %bitcast.64), calls=%async_computation.6 | async-start | bytes 524288 | tf_op jit(solution)/shard_map/all_to_all | solution.py:123
  87.9 0.8 copy.133
  88.7 5.2 %all-to-all-done.6 = bf16[4,128,256]{2,1,0:T(8,128)(2,1)S(1)} async-done(((bf16[4,128,256]{2,1,0:T(8,128)(2,1)}), bf16[4,128,256]{2,1,0:T(8,128)(2,1)S(1)}, u32[]{:S(2)}, u32[]{:S(2)}) %all-to-all-start.6) | async-done | bytes 262176 | tf_op jit(solution)/shard_map/all_to_all | solution.py:123
  93.9 3.4 %all-to-all-start.5 = ((bf16[4,128,256]{2,1,0:T(8,128)(2,1)}), bf16[4,128,256]{2,1,0:T(8,128)(2,1)S(1)}, u32[]{:S(2)}, u32[]{:S(2)}) async-start(bf16[4,128,256]{2,1,0:T(8,128)(2,1)} %bitcast.61), calls=%async_computation.5 | async-start | bytes 524288 | tf_op jit(solution)/shard_map/all_to_all | solution.py:116
  97.5 0.9 copy.137
  98.5 0.9 copy.139
  99.4 3.9 %all-to-all-done.5 = bf16[4,128,256]{2,1,0:T(8,128)(2,1)S(1)} async-done(((bf16[4,128,256]{2,1,0:T(8,128)(2,1)}), bf16[4,128,256]{2,1,0:T(8,128)(2,1)S(1)}, u32[]{:S(2)}, u32[]{:S(2)}) %all-to-all-start.5) | async-done | bytes 262176 | tf_op jit(solution)/shard_map/all_to_all | solution.py:116
  103.5 0.9 copy.138
  (79 shorter events, 6.6 us)
Async XLA Ops:
  0.6 5.6 %copy-start = (bf16[128,1024]{1,0:T(8,128)(2,1)S(1)}, bf16[128,1024]{1,0:T(8,128)(2,1)}, u32[]{:S(2)}) copy-start(bf16[128,1024]{1,0:T(8,128)(2,1)} %param.17) | copy-start | bytes 786436
  0.6 6.4 %copy-start.1 = (bf16[128,1024]{1,0:T(8,128)(2,1)S(1)}, bf16[128,1024]{1,0:T(8,128)(2,1)}, u32[]{:S(2)}) copy-start(bf16[128,1024]{1,0:T(8,128)(2,1)} %param.19) | copy-start | bytes 786436
  1.8 6.3 %copy-start.17 = (s32[4]{0:T(128)S(1)}, s32[4]{0:T(128)}, u32[]{:S(2)}) copy-start(s32[4]{0:T(128)} %param.21) | copy-start | bytes 52
  2.7 9.4 %all-to-all-start = ((bf16[128,4,256]{2,0,1:T(8,128)(2,1)}), bf16[128,4,256]{2,0,1:T(8,128)(2,1)S(1)}, u32[]{:S(2)}, u32[]{:S(2)}) async-start(bf16[128,4,256]{2,0,1:T(8,128)(2,1)} %copy.102), calls=%async_computation | async-start | bytes 524288 | tf_op jit(solution)/shard_map/all_to_all | solution.py:96
  6.2 18.9 %copy-start.2 = (bf16[128,1024]{1,0:T(8,128)(2,1)S(1)}, bf16[128,1024]{1,0:T(8,128)(2,1)}, u32[]{:S(2)}) copy-start(bf16[128,1024]{1,0:T(8,128)(2,1)} %param.20) | copy-start | bytes 786436
  12.1 9.4 %all-to-all-start.1 = ((bf16[128,4,256]{2,0,1:T(8,128)(2,1)}), bf16[128,4,256]{2,0,1:T(8,128)(2,1)S(1)}, u32[]{:S(2)}, u32[]{:S(2)}) async-start(bf16[128,4,256]{2,0,1:T(8,128)(2,1)} %copy.104), calls=%async_computation.1 | async-start | bytes 524288 | tf_op jit(solution)/shard_map/all_to_all | solution.py:97
  21.5 10.7 %all-to-all-start.2 = ((bf16[128,4,256]{0,2,1:T(8,128)(2,1)}), bf16[128,4,256]{0,2,1:T(8,128)(2,1)S(1)}, u32[]{:S(2)}, u32[]{:S(2)}) async-start(bf16[128,4,256]{0,2,1:T(8,128)(2,1)} %bitcast.9), calls=%async_computation.2 | async-start | bytes 524288 | tf_op jit(solution)/shard_map/all_to_all | solution.py:95
  26.4 15.3 %collective-permute-start = (bf16[64,512]{0,1:T(8,128)(2,1)S(1)}, bf16[64,512]{0,1:T(8,128)(2,1)S(1)}, u32[]{:S(2)}, u32[]{:S(2)}) collective-permute-start(bf16[64,512]{0,1:T(8,128)(2,1)S(1)} %get-tuple-element.101), channel_id=1, source_target_pairs={{0,4},{4,8},{8,12},{12,16},{16,20},{20,24},{24,28},{1,5},{5,9},{9,... | collective-permute-start | bytes 196616 | tf_op jit(solution)/shard_map/ppermute | solution.py:15
  27.7 14.0 %collective-permute-start.1 = (bf16[64,512]{0,1:T(8,128)(2,1)S(1)}, bf16[64,512]{0,1:T(8,128)(2,1)S(1)}, u32[]{:S(2)}, u32[]{:S(2)}) collective-permute-start(bf16[64,512]{0,1:T(8,128)(2,1)S(1)} %get-tuple-element.102), channel_id=1, source_target_pairs={{4,0},{8,4},{12,8},{16,12},{20,16},{24,20},{28,24},{5,1},{9,5},{13... | collective-permute-start | bytes 196616 | tf_op jit(solution)/shard_map/ppermute | solution.py:18
  32.2 9.4 %all-to-all-start.3 = ((bf16[128,4,256]{0,2,1:T(8,128)(2,1)}), bf16[128,4,256]{0,2,1:T(8,128)(2,1)S(1)}, u32[]{:S(2)}, u32[]{:S(2)}) async-start(bf16[128,4,256]{0,2,1:T(8,128)(2,1)} %bitcast.14), calls=%async_computation.3 | async-start | bytes 524288 | tf_op jit(solution)/shard_map/all_to_all | solution.py:98
  35.7 14.4 %copy-start.12 = (bf16[1,128,256]{1,2,0:T(8,128)(2,1)}, bf16[1,128,256]{1,2,0:T(8,128)(2,1)S(1)}, u32[]{:S(2)}) copy-start(bf16[1,128,256]{1,2,0:T(8,128)(2,1)S(1)} %get-tuple-element.105) | copy-start | bytes 196612
  35.7 15.7 %copy-start.10 = (bf16[1,128,256]{1,2,0:T(8,128)(2,1)}, bf16[1,128,256]{1,2,0:T(8,128)(2,1)S(1)}, u32[]{:S(2)}) copy-start(bf16[1,128,256]{1,2,0:T(8,128)(2,1)S(1)} %get-tuple-element.106) | copy-start | bytes 196612
  42.3 7.9 %copy-start.7 = (bf16[256,256]{0,1:T(8,128)(2,1)}, bf16[256,256]{0,1:T(8,128)(2,1)S(1)}, u32[]{:S(2)}) copy-start(bf16[256,256]{0,1:T(8,128)(2,1)S(1)} %get-tuple-element.111) | copy-start | bytes 393220
  47.4 1.6 %copy-start.16 = (pred[128,256]{0,1:T(8,128)(4,1)S(1)}, pred[128,256]{0,1:T(8,128)(4,1)}, u32[]{:S(2)}) copy-start(pred[128,256]{0,1:T(8,128)(4,1)} %fusion.85) | copy-start | bytes 98308
  50.1 0.9 copy-start.15
  51.4 2.8 %copy-start.18 = (f32[4,128,256]{1,2,0:T(8,128)}, f32[4,128,256]{1,2,0:T(8,128)S(1)}, u32[]{:S(2)}) copy-start(f32[4,128,256]{1,2,0:T(8,128)S(1)} %get-tuple-element.120) | copy-start | bytes 1572868
  51.4 1.3 %copy-start.13 = (bf16[1,128,256]{1,2,0:T(8,128)(2,1)S(1)}, bf16[1,128,256]{1,2,0:T(8,128)(2,1)}, u32[]{:S(2)}) copy-start(bf16[1,128,256]{1,2,0:T(8,128)(2,1)} %copy-done.12) | copy-start | bytes 196612
  52.7 1.6 %copy-start.11 = (bf16[1,128,256]{1,2,0:T(8,128)(2,1)S(1)}, bf16[1,128,256]{1,2,0:T(8,128)(2,1)}, u32[]{:S(2)}) copy-start(bf16[1,128,256]{1,2,0:T(8,128)(2,1)} %copy-done.10) | copy-start | bytes 196612
  55.3 0.9 copy-start.3
  55.3 1.0 copy-start.4
  56.3 0.9 copy-start.5
  56.3 1.0 copy-start.6
  57.3 1.6 %copy-start.8 = (bf16[256,256]{0,1:T(8,128)(2,1)S(1)}, bf16[256,256]{0,1:T(8,128)(2,1)}, u32[]{:S(2)}) copy-start(bf16[256,256]{0,1:T(8,128)(2,1)} %copy-done.7) | copy-start | bytes 393220
  57.6 9.7 %collective-permute-start.2 = (f32[64,512]{0,1:T(8,128)S(1)}, f32[64,512]{0,1:T(8,128)S(1)}, u32[]{:S(2)}, u32[]{:S(2)}) collective-permute-start(f32[64,512]{0,1:T(8,128)S(1)} %slice.255), channel_id=1, source_target_pairs={{0,4},{4,8},{8,12},{12,16},{16,20},{20,24},{24,28},{1,5},{5,9},{9,... | collective-permute-start | bytes 393224 | tf_op jit(solution)/shard_map/ppermute | solution.py:26
  67.5 12.9 %collective-permute-start.3 = (f32[64,512]{0,1:T(8,128)S(1)}, f32[64,512]{0,1:T(8,128)S(1)}, u32[]{:S(2)}, u32[]{:S(2)}) collective-permute-start(f32[64,512]{0,1:T(8,128)S(1)} %get-tuple-element.91), channel_id=1, source_target_pairs={{4,0},{8,4},{12,8},{16,12},{20,16},{24,20},{28,24},{5,1},{9,5},{13... | collective-permute-start | bytes 393224 | tf_op jit(solution)/shard_map/ppermute | solution.py:26
  73.3 0.8 copy-start.9
  73.3 0.9 copy-start.14
  75.0 9.4 %all-to-all-start.4 = ((bf16[4,128,256]{2,1,0:T(8,128)(2,1)}), bf16[4,128,256]{2,1,0:T(8,128)(2,1)S(1)}, u32[]{:S(2)}, u32[]{:S(2)}) async-start(bf16[4,128,256]{2,1,0:T(8,128)(2,1)} %bitcast.42), calls=%async_computation.4 | async-start | bytes 524288 | tf_op jit(solution)/shard_map/all_to_all | solution.py:113
  84.5 9.4 %all-to-all-start.6 = ((bf16[4,128,256]{2,1,0:T(8,128)(2,1)}), bf16[4,128,256]{2,1,0:T(8,128)(2,1)S(1)}, u32[]{:S(2)}, u32[]{:S(2)}) async-start(bf16[4,128,256]{2,1,0:T(8,128)(2,1)} %bitcast.64), calls=%async_computation.6 | async-start | bytes 524288 | tf_op jit(solution)/shard_map/all_to_all | solution.py:123
  93.9 9.4 %all-to-all-start.5 = ((bf16[4,128,256]{2,1,0:T(8,128)(2,1)}), bf16[4,128,256]{2,1,0:T(8,128)(2,1)S(1)}, u32[]{:S(2)}, u32[]{:S(2)}) async-start(bf16[4,128,256]{2,1,0:T(8,128)(2,1)} %bitcast.61), calls=%async_computation.5 | async-start | bytes 524288 | tf_op jit(solution)/shard_map/all_to_all | solution.py:116
where the time goes:
time: 105 us; the launch traced here: 104 us
  starting transfers between devices  35.2 us (34%)
  waiting for transfers between devices  31.4 us (30%)
  local copies, waits for them, and re-layouts  16.8 us (16%)
  matrix products  15.9 us (15%)
  other arithmetic  3.8 us (4%)
  between operations  1.16 us (1%)
    ppermute x2, waiting for transfers between devices, shifted(): return lax.ppermute(block, axis, route)  6.94 us
    unnamed x43, local copies, waits for them, and re-layouts  6.22 us
    all_to_all x1, waiting for transfers between devices, body(): lax.all_to_all(grad_output, 'head', split_axis=1, concat_axis=0, tiled=True)  5.95 us
    ppermute x2, starting transfers between devices, shifted(): return lax.ppermute(block, axis, route)  5.54 us
    all_to_all x1, waiting for transfers between devices, body(): lax.all_to_all(value_vectors, 'head', split_axis=1, concat_axis=0, tiled=...  5.22 us
    all_to_all x1, waiting for transfers between devices, body(): lax.all_to_all(own_rows[:, columns:].astype(jnp.bfloat16), 'head', split_...  5.16 us
    dot_general x4, matrix products, band_grads(): jnp.einsum('hqk,khd->qhd', score_grad, key_block, preferred_element_type=...  4.84 us
    ppermute x1, starting transfers between devices, with_halo(): lax.ppermute(lax.slice_in_dim(block, 0, width, axis=dim), axis, backward)  4.55 us
  transfers between devices with their start and end apart: 11, of which 7 were waited for; matrix products, arithmetic and copies ran while one was open for 16% of the time, Pallas kernels for 0%

commit v1 on v0

--- a/solution.py
+++ b/solution.py
@@ -5,6 +5,22 @@
 
 DH = 64
 WIN = 64
+
+
+def pairwise_exchange(array, axis, split, join):
+    ways, here = (lax.axis_size(axis), lax.axis_index(axis))
+    width = array.shape[split] // ways
+    dims = list(array.shape)
+    dims[split] = width
+    height = dims[join]
+    dims[join] = height * ways
+    full = jnp.zeros(dims, array.dtype)
+    for mask in range(ways):
+        part = lax.dynamic_slice_in_dim(array, (here ^ mask) * width, width, axis=split)
+        if mask:
+            part = lax.ppermute(part, axis, [(d, d ^ mask) for d in range(ways)])
+        full = lax.dynamic_update_slice_in_dim(full, part, (here ^ mask) * height, axis=join)
+    return full
 
 
 def with_halo(block, sides, width):
@@ -120,13 +136,7 @@
             concat_axis=1,
             tiled=True,
         ),
-        lax.all_to_all(
-            own_rows[:, columns:].astype(jnp.bfloat16),
-            "head",
-            split_axis=0,
-            concat_axis=1,
-            tiled=True,
-        ),
+        pairwise_exchange(own_rows[:, columns:].astype(jnp.bfloat16), "head", 0, 1),
     )
     return (outputs[0], outputs[1], outputs[2])
 

time: 105 us -> 93.8 us (0.89)
  local copies, waits for them, and re-layouts: 16.8 us -> 10.6 us
  waiting for transfers between devices: 31.4 us -> 28.2 us
  matrix products: 15.9 us -> 13.8 us
    ppermute x0 -> x3, waiting for transfers between devices: none -> 6.68 us  [pairwise_exchange(): part = lax.ppermute(part, axis, [(d, d ^ mask) for d in range(ways)])]
    all_to_all x1 -> x0, waiting for transfers between devices: 5.16 us -> none  [body(): lax.all_to_all(own_rows[:, columns:].astype(jnp.bfloat16), 'head', split_...]
    all_to_all x1, waiting for transfers between devices: 3.94 us -> 0.01 us  [body(): lax.all_to_all(own_rows[:, :columns].astype(jnp.bfloat16), 'head', split_...]
    unnamed x43 -> x35, local copies, waits for them, and re-layouts: 6.22 us -> 2.51 us
    all_to_all x1 -> x0, starting transfers between devices: 3.41 us -> none  [body(): lax.all_to_all(own_rows[:, columns:].astype(jnp.bfloat16), 'head', split_...]
    scatter-add x2 -> x0, local copies, waits for them, and re-layouts: 3.37 us -> none  [body(): own_rows.at[:WIN].add(arrived[0]).at[block_rows - WIN:].add(arrived[1])]
    ppermute x2, waiting for transfers between devices: 6.94 us -> 3.71 us  [shifted(): return lax.ppermute(block, axis, route)]
    all_to_all x1, waiting for transfers between devices: 1.49 us -> 4.55 us  [body(): lax.all_to_all(query_grad.astype(jnp.bfloat16), 'head', split_axis=0, con...]
  transfers between devices with their start and end apart: 11 -> 13, of which waited for: 7 -> 6; matrix products, arithmetic and copies ran while one was open for 16% -> 14% of each run, Pallas kernels for 0% -> 0%
where the time goes in v1:
time: 93.8 us; the launch traced here: 92.9 us
  starting transfers between devices  34.7 us (37%)
  waiting for transfers between devices  28.2 us (30%)
  matrix products  13.8 us (15%)
  local copies, waits for them, and re-layouts  10.6 us (11%)
  other arithmetic  4.36 us (5%)
  between operations  1.27 us (1%)
    ppermute x3, waiting for transfers between devices, pairwise_exchange(): part = lax.ppermute(part, axis, [(d, d ^ mask) for d in range(ways)])  6.68 us
    ppermute x2, starting transfers between devices, shifted(): return lax.ppermute(block, axis, route)  5.8 us
    dot_general x4, matrix products, band_grads(): jnp.einsum('hqk,khd->qhd', score_grad, key_block, preferred_element_type=...  5.55 us
    all_to_all x1, waiting for transfers between devices, body(): lax.all_to_all(grad_output, 'head', split_axis=1, concat_axis=0, tiled=True)  5.33 us
    all_to_all x1, waiting for transfers between devices, body(): lax.all_to_all(value_vectors, 'head', split_axis=1, concat_axis=0, tiled=...  5.23 us
    ppermute x1, starting transfers between devices, with_halo(): lax.ppermute(lax.slice_in_dim(block, 0, width, axis=dim), axis, backward)  4.55 us
    all_to_all x1, waiting for transfers between devices, body(): lax.all_to_all(query_grad.astype(jnp.bfloat16), 'head', split_axis=0, con...  4.55 us
    ppermute x2, waiting for transfers between devices, shifted(): return lax.ppermute(block, axis, route)  3.71 us
  transfers between devices with their start and end apart: 13, of which 6 were waited for; matrix products, arithmetic and copies ran while one was open for 14% of the time, Pallas kernels for 0%

profile of v1, /device:TPU:26, one launch (start us, length us, event | category | flops | bytes accessed | tf_op | source)
XLA Modules:
  0.0 92.9 jit_solution(5158475037763423554)
XLA Ops:
  0.7 1.2 %copy.118 = bf16[128,1024]{0,1:T(8,128)(2,1)S(1)} copy(bf16[128,1024]{1,0:T(8,128)(2,1)} %param.18) | data formatting | bytes 524288 | tf_op args[1]
  1.8 0.9 copy.119
  2.7 3.4 %all-to-all-start = ((bf16[128,4,256]{2,0,1:T(8,128)(2,1)}), bf16[128,4,256]{2,0,1:T(8,128)(2,1)S(1)}, u32[]{:S(2)}, u32[]{:S(2)}) async-start(bf16[128,4,256]{2,0,1:T(8,128)(2,1)} %copy.119), calls=%async_computation | async-start | bytes 524288 | tf_op jit(solution)/shard_map/all_to_all | solution.py:112
  6.2 0.8 copy.176
  7.2 0.9 copy.121
  8.6 0.8 fusion.88
  9.4 2.7 %all-to-all-done = bf16[128,4,256]{2,0,1:T(8,128)(2,1)S(1)} async-done(((bf16[128,4,256]{2,0,1:T(8,128)(2,1)}), bf16[128,4,256]{2,0,1:T(8,128)(2,1)S(1)}, u32[]{:S(2)}, u32[]{:S(2)}) %all-to-all-start) | async-done | bytes 262176 | tf_op jit(solution)/shard_map/all_to_all | solution.py:112
  12.1 3.4 %all-to-all-start.1 = ((bf16[128,4,256]{2,0,1:T(8,128)(2,1)}), bf16[128,4,256]{2,0,1:T(8,128)(2,1)S(1)}, u32[]{:S(2)}, u32[]{:S(2)}) async-start(bf16[128,4,256]{2,0,1:T(8,128)(2,1)} %copy.121), calls=%async_computation.1 | async-start | bytes 524288 | tf_op jit(solution)/shard_map/all_to_all | solution.py:113
  15.5 0.8 fusion.87
  16.3 5.2 %all-to-all-done.1 = bf16[128,4,256]{2,0,1:T(8,128)(2,1)S(1)} async-done(((bf16[128,4,256]{2,0,1:T(8,128)(2,1)}), bf16[128,4,256]{2,0,1:T(8,128)(2,1)S(1)}, u32[]{:S(2)}, u32[]{:S(2)}) %all-to-all-start.1) | async-done | bytes 262176 | tf_op jit(solution)/shard_map/all_to_all | solution.py:113
  21.5 3.4 %all-to-all-start.2 = ((bf16[128,4,256]{0,2,1:T(8,128)(2,1)}), bf16[128,4,256]{0,2,1:T(8,128)(2,1)S(1)}, u32[]{:S(2)}, u32[]{:S(2)}) async-start(bf16[128,4,256]{0,2,1:T(8,128)(2,1)} %bitcast.9), calls=%async_computation.2 | async-start | bytes 524288 | tf_op jit(solution)/shard_map/all_to_all | solution.py:111
  25.1 0.8 copy.177
  26.4 1.3 %collective-permute-start = (bf16[64,512]{0,1:T(8,128)(2,1)S(1)}, bf16[64,512]{0,1:T(8,128)(2,1)S(1)}, u32[]{:S(2)}, u32[]{:S(2)}) collective-permute-start(bf16[64,512]{0,1:T(8,128)(2,1)S(1)} %get-tuple-element.101), channel_id=1, source_target_pairs={{0,4},{4,8},{8,12},{12,16},{16,20},{20,24},{24,28},{1,5},{5,9},{9,... | collective-permute-start | bytes 196616 | tf_op jit(solution)/shard_map/ppermute | solution.py:31
  27.7 4.6 %collective-permute-start.1 = (bf16[64,512]{0,1:T(8,128)(2,1)S(1)}, bf16[64,512]{0,1:T(8,128)(2,1)S(1)}, u32[]{:S(2)}, u32[]{:S(2)}) collective-permute-start(bf16[64,512]{0,1:T(8,128)(2,1)S(1)} %get-tuple-element.102), channel_id=1, source_target_pairs={{4,0},{8,4},{12,8},{16,12},{20,16},{24,20},{28,24},{5,1},{9,5},{13... | collective-permute-start | bytes 196616 | tf_op jit(solution)/shard_map/ppermute | solution.py:34
  32.3 3.4 %all-to-all-start.3 = ((bf16[128,4,256]{0,2,1:T(8,128)(2,1)}), bf16[128,4,256]{0,2,1:T(8,128)(2,1)S(1)}, u32[]{:S(2)}, u32[]{:S(2)}) async-start(bf16[128,4,256]{0,2,1:T(8,128)(2,1)} %bitcast.14), calls=%async_computation.3 | async-start | bytes 524288 | tf_op jit(solution)/shard_map/all_to_all | solution.py:114
  35.7 0.7 fusion.120
  36.4 5.3 %all-to-all-done.3 = bf16[128,4,256]{0,2,1:T(8,128)(2,1)S(1)} async-done(((bf16[128,4,256]{0,2,1:T(8,128)(2,1)}), bf16[128,4,256]{0,2,1:T(8,128)(2,1)S(1)}, u32[]{:S(2)}, u32[]{:S(2)}) %all-to-all-start.3) | async-done | bytes 262176 | tf_op jit(solution)/shard_map/all_to_all | solution.py:114
  41.7 1.2 %pad_maximum_fusion.5 = (bf16[256,256]{0,1:T(8,128)(2,1)S(1)}, bf16[256,256]{0,1:T(8,128)(2,1)S(1)}, bf16[256,256]{0,1:T(8,128)(2,1)S(1)}, bf16[256,256]{0,1:T(8...) fusion(bf16[64,512]{0,1:T(8,128)(2,1)S(1)} %collective-permute-, ...), kind=kLoop, calls=%fused_computation.104 | loop fusion | flops 1572864 | bytes 2359296 | tf_op jit(solution)/shard_map/concatenate | solution.py:35
  43.2 0.4 fusion.125
  43.6 0.9 convolution_convert_fusion.3
  44.5 0.3 fusion.42
  44.8 0.6 fusion.70
  45.7 0.4 fusion.122
  46.1 0.9 convolution_convert_fusion.2
  47.0 0.3 fusion.45
  47.3 0.6 fusion.64
  48.8 0.4 fusion.123
  49.2 0.6 fusion.66
  50.0 0.3 fusion.44
  50.9 1.2 %fusion.124 = (f32[4,128]{1,0:T(4,128)S(1)}, f32[4,128,256]{1,2,0:T(8,128)}) fusion(bf16[128,4,64]{0,2,1:T(8,128)(2,1)S(1)} %bitcast.184, bf16[256,4,64]{0,2,1:T(8,128)(2,1)S(1)} %bitcast.171, pred[128,256]{0,1:T(8,128)(4,1)S(1)} %copy-done.12), kind=kOutput, calls=%fused_computation.182 | convolution fusion | flops 17432832 | bytes 755712 | tf_op jit(solution)/shard_map/sub | solution.py:80
  52.0 0.6 fusion.68
  52.8 1.5 %fusion.43 = f32[4,256,64]{1,2,0:T(8,128)S(1)} fusion(bf16[128,4,64]{0,2,1:T(8,128)(2,1)S(1)} %bitcast.186, f32[4,128,256]{1,2,0:T(8,128)S(1)} %fusion.126, f32[4,128,256]{1,2,0:T(8,128)} %get-tuple-element.124, f32[4,128]{1,0:T(4,128)S(1)} %get-tuple-element.123), kind=kOutput, calls=%fused_computation.55 | convolution fusion | flops 17695488 | bytes 1378304 | tf_op jit(solution)/shard_map/hqk,qhd->khd/dot_general | solution.py:94
  55.1 1.4 %collective-permute-start.2 = (f32[64,512]{1,0:T(8,128)S(1)}, f32[64,512]{1,0:T(8,128)S(1)}, u32[]{:S(2)}, u32[]{:S(2)}) collective-permute-start(f32[64,512]{1,0:T(8,128)S(1)} %slice.255), channel_id=1, source_target_pairs={{0,4},{4,8},{8,12},{12,16},{16,20},{20,24},{24,28},{1,5},{5,9},{9,... | collective-permute-start | bytes 393224 | tf_op jit(solution)/shard_map/ppermute | solution.py:42
  56.7 1.8 %convolution_convert_fusion = bf16[4,128,64]{1,2,0:T(8,128)(2,1)S(1)} fusion(bf16[256,4,64]{0,2,1:T(8,128)(2,1)S(1)} %bitcast.176, f32[4,128,256]{1,2,0:T(8,128)} %copy-done.1, f32[4,128,256]{1,2,0:T(8,128)} %copy-done.15, f32[4,128]{1,0:T(4,128)S(1)} %get-tuple-element.121), kind=kOutput, calls=%fused_computation.50 | convolution fusion | flops 17728256 | bytes 1247232 | tf_op jit(solution)/shard_map/hqk,khd->qhd/dot_general | solution.py:91
  58.5 3.7 %collective-permute-done.2 = f32[64,512]{1,0:T(8,128)S(1)} collective-permute-done((f32[64,512]{1,0:T(8,128)S(1)}, f32[64,512]{1,0:T(8,128)S(1)}, u32[]{:S(2)}, u32[]{:S(2)}) %collective-permute-start.2) | collective-permute-done | bytes 131104 | tf_op jit(solution)/shard_map/ppermute | solution.py:42
  62.2 4.4 %collective-permute-start.3 = (f32[64,512]{1,0:T(8,128)S(1)}, f32[64,512]{1,0:T(8,128)S(1)}, u32[]{:S(2)}, u32[]{:S(2)}) collective-permute-start(f32[64,512]{1,0:T(8,128)S(1)} %get-tuple-element.91), channel_id=1, source_target_pairs={{4,0},{8,4},{12,8},{16,12},{20,16},{24,20},{28,24},{5,1},{9,5},{13... | collective-permute-start | bytes 393224 | tf_op jit(solution)/shard_map/ppermute | solution.py:42
  66.6 1.9 %convolution_convert_fusion.1 = bf16[4,128,64]{1,2,0:T(8,128)(2,1)S(1)} fusion(bf16[256,4,64]{0,2,1:T(8,128)(2,1)S(1)} %bitcast.173, f32[4,128,256]{1,2,0:T(8,128)} %copy-done, f32[4,128,256]{1,2,0:T(8,128)} %get-tuple-element.124, f32[4,128]{1,0:T(4,128)S(1)} %get-tuple-element.123), kind=kOutput, calls=%fused_computation.51 | convolution fusion | flops 17728256 | bytes 1247232 | tf_op jit(solution)/shard_map/hqk,khd->qhd/dot_general | solution.py:91
  68.6 0.8 copy.140
  69.4 3.4 %all-to-all-start.4 = ((bf16[4,128,256]{2,1,0:T(8,128)(2,1)}), bf16[4,128,256]{2,1,0:T(8,128)(2,1)S(1)}, u32[]{:S(2)}, u32[]{:S(2)}) async-start(bf16[4,128,256]{2,1,0:T(8,128)(2,1)} %bitcast.42), calls=%async_computation.4 | async-start | bytes 524288 | tf_op jit(solution)/shard_map/all_to_all | solution.py:129
  73.0 0.7 fusion.119
  73.8 0.5 collective-permute-start.4
  74.3 4.5 %all-to-all-done.4 = bf16[4,128,256]{2,1,0:T(8,128)(2,1)S(1)} async-done(((bf16[4,128,256]{2,1,0:T(8,128)(2,1)}), bf16[4,128,256]{2,1,0:T(8,128)(2,1)S(1)}, u32[]{:S(2)}, u32[]{:S(2)}) %all-to-all-start.4) | async-done | bytes 262176 | tf_op jit(solution)/shard_map/all_to_all | solution.py:129
  79.0 0.9 copy.159
  79.9 3.4 %all-to-all-start.5 = ((bf16[4,128,256]{2,1,0:T(8,128)(2,1)}), bf16[4,128,256]{2,1,0:T(8,128)(2,1)S(1)}, u32[]{:S(2)}, u32[]{:S(2)}) async-start(bf16[4,128,256]{2,1,0:T(8,128)(2,1)} %bitcast.61), calls=%async_computation.5 | async-start | bytes 524288 | tf_op jit(solution)/shard_map/all_to_all | solution.py:132
  83.3 1.7 %collective-permute-start.6 = (bf16[128,256]{1,0:T(8,128)(2,1)S(1)}, bf16[128,256]{1,0:T(8,128)(2,1)S(1)}, u32[]{:S(2)}, u32[]{:S(2)}) collective-permute-start(bf16[128,256]{1,0:T(8,128)(2,1)S(1)} %get-tuple-element.103), channel_id=1, source_target_pairs={{0,3},{1,2},{2,1},{3,0},{4,7},{5,6},{6,5},{7,4},{8,11},{9,10},{10,... | collective-permute-start | bytes 196616 | tf_op jit(solution)/shard_map/ppermute | solution.py:21
  85.0 0.4 collective-permute-start.5
  85.4 6.7 %collective-permute-done.5 = bf16[128,256]{1,0:T(8,128)(2,1)S(1)} collective-permute-done((bf16[128,256]{1,0:T(8,128)(2,1)S(1)}, bf16[128,256]{1,0:T(8,128)(2,1)S(1)}, u32[]{:S(2)}, u32[]{:S(2)}) %collective-permute-start.5) | collective-permute-done | bytes 65568 | tf_op jit(solution)/shard_map/ppermute | solution.py:21
  92.2 0.8 copy.178
  (83 shorter events, 4.9 us)
Async XLA Ops:
  0.6 5.6 %copy-start.2 = (bf16[128,1024]{1,0:T(8,128)(2,1)S(1)}, bf16[128,1024]{1,0:T(8,128)(2,1)}, u32[]{:S(2)}) copy-start(bf16[128,1024]{1,0:T(8,128)(2,1)} %param.17) | copy-start | bytes 786436
  0.6 6.4 %copy-start.3 = (bf16[128,1024]{1,0:T(8,128)(2,1)S(1)}, bf16[128,1024]{1,0:T(8,128)(2,1)}, u32[]{:S(2)}) copy-start(bf16[128,1024]{1,0:T(8,128)(2,1)} %param.19) | copy-start | bytes 786436
  1.8 6.3 %copy-start.14 = (s32[4]{0:T(128)S(1)}, s32[4]{0:T(128)}, u32[]{:S(2)}) copy-start(s32[4]{0:T(128)} %param.21) | copy-start | bytes 52
  2.7 9.4 %all-to-all-start = ((bf16[128,4,256]{2,0,1:T(8,128)(2,1)}), bf16[128,4,256]{2,0,1:T(8,128)(2,1)S(1)}, u32[]{:S(2)}, u32[]{:S(2)}) async-start(bf16[128,4,256]{2,0,1:T(8,128)(2,1)} %copy.119), calls=%async_computation | async-start | bytes 524288 | tf_op jit(solution)/shard_map/all_to_all | solution.py:112
  6.2 18.9 %copy-start.4 = (bf16[128,1024]{1,0:T(8,128)(2,1)S(1)}, bf16[128,1024]{1,0:T(8,128)(2,1)}, u32[]{:S(2)}) copy-start(bf16[128,1024]{1,0:T(8,128)(2,1)} %param.20) | copy-start | bytes 786436
  12.1 9.4 %all-to-all-start.1 = ((bf16[128,4,256]{2,0,1:T(8,128)(2,1)}), bf16[128,4,256]{2,0,1:T(8,128)(2,1)S(1)}, u32[]{:S(2)}, u32[]{:S(2)}) async-start(bf16[128,4,256]{2,0,1:T(8,128)(2,1)} %copy.121), calls=%async_computation.1 | async-start | bytes 524288 | tf_op jit(solution)/shard_map/all_to_all | solution.py:113
  21.5 10.7 %all-to-all-start.2 = ((bf16[128,4,256]{0,2,1:T(8,128)(2,1)}), bf16[128,4,256]{0,2,1:T(8,128)(2,1)S(1)}, u32[]{:S(2)}, u32[]{:S(2)}) async-start(bf16[128,4,256]{0,2,1:T(8,128)(2,1)} %bitcast.9), calls=%async_computation.2 | async-start | bytes 524288 | tf_op jit(solution)/shard_map/all_to_all | solution.py:111
  26.4 15.3 %collective-permute-start = (bf16[64,512]{0,1:T(8,128)(2,1)S(1)}, bf16[64,512]{0,1:T(8,128)(2,1)S(1)}, u32[]{:S(2)}, u32[]{:S(2)}) collective-permute-start(bf16[64,512]{0,1:T(8,128)(2,1)S(1)} %get-tuple-element.101), channel_id=1, source_target_pairs={{0,4},{4,8},{8,12},{12,16},{16,20},{20,24},{24,28},{1,5},{5,9},{9,... | collective-permute-start | bytes 196616 | tf_op jit(solution)/shard_map/ppermute | solution.py:31
  27.7 14.0 %collective-permute-start.1 = (bf16[64,512]{0,1:T(8,128)(2,1)S(1)}, bf16[64,512]{0,1:T(8,128)(2,1)S(1)}, u32[]{:S(2)}, u32[]{:S(2)}) collective-permute-start(bf16[64,512]{0,1:T(8,128)(2,1)S(1)} %get-tuple-element.102), channel_id=1, source_target_pairs={{4,0},{8,4},{12,8},{16,12},{20,16},{24,20},{28,24},{5,1},{9,5},{13... | collective-permute-start | bytes 196616 | tf_op jit(solution)/shard_map/ppermute | solution.py:34
  32.3 9.4 %all-to-all-start.3 = ((bf16[128,4,256]{0,2,1:T(8,128)(2,1)}), bf16[128,4,256]{0,2,1:T(8,128)(2,1)S(1)}, u32[]{:S(2)}, u32[]{:S(2)}) async-start(bf16[128,4,256]{0,2,1:T(8,128)(2,1)} %bitcast.14), calls=%async_computation.3 | async-start | bytes 524288 | tf_op jit(solution)/shard_map/all_to_all | solution.py:114
  47.9 0.9 copy-start.6
  47.9 0.9 copy-start.11
  47.9 0.9 copy-start.13
  48.7 1.2 %copy-start.1 = (f32[4,128,256]{1,2,0:T(8,128)}, f32[4,128,256]{1,2,0:T(8,128)S(1)}, u32[]{:S(2)}) copy-start(f32[4,128,256]{1,2,0:T(8,128)S(1)} %fusion.127) | copy-start | bytes 1572868
  49.2 0.8 copy-start.15
  50.0 0.8 copy-start.9
  50.0 0.8 copy-start.12
  50.7 2.0 %copy-start = (f32[4,128,256]{1,2,0:T(8,128)}, f32[4,128,256]{1,2,0:T(8,128)S(1)}, u32[]{:S(2)}) copy-start(f32[4,128,256]{1,2,0:T(8,128)S(1)} %fusion.126) | copy-start | bytes 1572868
  55.1 1.5 %copy-start.7 = (bf16[256,256]{0,1:T(8,128)(2,1)S(1)}, bf16[256,256]{0,1:T(8,128)(2,1)}, u32[]{:S(2)}) copy-start(bf16[256,256]{0,1:T(8,128)(2,1)} %get-tuple-element.115) | copy-start | bytes 393220
  55.1 7.1 %collective-permute-start.2 = (f32[64,512]{1,0:T(8,128)S(1)}, f32[64,512]{1,0:T(8,128)S(1)}, u32[]{:S(2)}, u32[]{:S(2)}) collective-permute-start(f32[64,512]{1,0:T(8,128)S(1)} %slice.255), channel_id=1, source_target_pairs={{0,4},{4,8},{8,12},{12,16},{16,20},{20,24},{24,28},{1,5},{5,9},{9,... | collective-permute-start | bytes 393224 | tf_op jit(solution)/shard_map/ppermute | solution.py:42
  62.2 6.3 %copy-start.8 = (bf16[4,64,128]{2,1,0:T(8,128)(2,1)S(1)}, bf16[4,64,128]{2,1,0:T(8,128)(2,1)}, u32[]{:S(2)}) copy-start(bf16[4,64,128]{2,1,0:T(8,128)(2,1)} %convolution_convert_fusion.3) | copy-start | bytes 196612
  62.2 6.3 %copy-start.10 = (bf16[4,64,128]{2,1,0:T(8,128)(2,1)S(1)}, bf16[4,64,128]{2,1,0:T(8,128)(2,1)}, u32[]{:S(2)}) copy-start(bf16[4,64,128]{2,1,0:T(8,128)(2,1)} %convolution_convert_fusion.2) | copy-start | bytes 196612
  62.2 10.6 %collective-permute-start.3 = (f32[64,512]{1,0:T(8,128)S(1)}, f32[64,512]{1,0:T(8,128)S(1)}, u32[]{:S(2)}, u32[]{:S(2)}) collective-permute-start(f32[64,512]{1,0:T(8,128)S(1)} %get-tuple-element.91), channel_id=1, source_target_pairs={{4,0},{8,4},{12,8},{16,12},{20,16},{24,20},{28,24},{5,1},{9,5},{13... | collective-permute-start | bytes 393224 | tf_op jit(solution)/shard_map/ppermute | solution.py:42
  69.4 9.4 %all-to-all-start.4 = ((bf16[4,128,256]{2,1,0:T(8,128)(2,1)}), bf16[4,128,256]{2,1,0:T(8,128)(2,1)S(1)}, u32[]{:S(2)}, u32[]{:S(2)}) async-start(bf16[4,128,256]{2,1,0:T(8,128)(2,1)} %bitcast.42), calls=%async_computation.4 | async-start | bytes 524288 | tf_op jit(solution)/shard_map/all_to_all | solution.py:129
  73.8 11.6 %collective-permute-start.4 = (bf16[128,256]{1,0:T(8,128)(2,1)S(1)}, bf16[128,256]{1,0:T(8,128)(2,1)S(1)}, u32[]{:S(2)}, u32[]{:S(2)}) collective-permute-start(bf16[128,256]{1,0:T(8,128)(2,1)S(1)} %get-tuple-element.105), channel_id=1, source_target_pairs={{0,1},{1,0},{2,3},{3,2},{4,5},{5,4},{6,7},{7,6},{8,9},{9,8},{10,11... | collective-permute-start | bytes 196616 | tf_op jit(solution)/shard_map/ppermute | solution.py:21
  79.9 12.3 %all-to-all-start.5 = ((bf16[4,128,256]{2,1,0:T(8,128)(2,1)}), bf16[4,128,256]{2,1,0:T(8,128)(2,1)S(1)}, u32[]{:S(2)}, u32[]{:S(2)}) async-start(bf16[4,128,256]{2,1,0:T(8,128)(2,1)} %bitcast.61), calls=%async_computation.5 | async-start | bytes 524288 | tf_op jit(solution)/shard_map/all_to_all | solution.py:132
  83.3 8.8 %collective-permute-start.6 = (bf16[128,256]{1,0:T(8,128)(2,1)S(1)}, bf16[128,256]{1,0:T(8,128)(2,1)S(1)}, u32[]{:S(2)}, u32[]{:S(2)}) collective-permute-start(bf16[128,256]{1,0:T(8,128)(2,1)S(1)} %get-tuple-element.103), channel_id=1, source_target_pairs={{0,3},{1,2},{2,1},{3,0},{4,7},{5,6},{6,5},{7,4},{8,11},{9,10},{10,... | collective-permute-start | bytes 196616 | tf_op jit(solution)/shard_map/ppermute | solution.py:21
  85.0 7.1 %collective-permute-start.5 = (bf16[128,256]{1,0:T(8,128)(2,1)S(1)}, bf16[128,256]{1,0:T(8,128)(2,1)S(1)}, u32[]{:S(2)}, u32[]{:S(2)}) collective-permute-start(bf16[128,256]{1,0:T(8,128)(2,1)S(1)} %get-tuple-element.104), channel_id=1, source_target_pairs={{0,2},{1,3},{2,0},{3,1},{4,6},{5,7},{6,4},{7,5},{8,10},{9,11},{10,... | collective-permute-start | bytes 196616 | tf_op jit(solution)/shard_map/ppermute | solution.py:21
  92.1 0.8 copy-start.5
